TPU v7x, 768 devices: a whole 4x8x12 slice. The times are simulated.
768 devices in a mesh: outer: 6 (over z_lo), dp: 128 (over x, z_hi, y, core).
Axes of the slice: x: 4, y: 8, z: 12 (z_hi: 2, z_lo: 6; z = z_hi * 6 + z_lo), core: 2. Of those that a mesh axis runs over, the one named last changes fastest.
Arguments:
- grads: float32 [6, 6, 1024, 576], P('outer', None, 'dp'), may hold values from -64 to 64
- momentum: float32 [6, 1024, 576], P(None, 'dp'), may hold values from -4 to 4
Outputs:
- momentum_new: float32 [6, 1024, 576], P(None, 'dp')
- update: float32 [6, 1024, 576], P(None, 'dp')
All inputs are finite; a program needn't handle non-finite values.
Results may differ from a plain program's by a relative error of at most 0.0057.
Values may be sent and summed in bfloat16 or wider, within the bound.
A program may use at most 32 MiB of HBM per device.

v0:
```python
import math

import jax
import jax.numpy as jnp
from jax import lax
from jax.sharding import PartitionSpec as P

ITERS = 2


coef_a = 3.4445
coef_b = -4.775
coef_c = 2.0315
momentum_rate = 0.95
epsilon = 1e-06


def broadcast(value, axis, source):
    kept = jnp.where(lax.axis_index(axis) == source, value, 0).astype(value.dtype)
    return lax.psum(kept, axis)


def gram_product(matrix):
    return lax.dot_general(
        matrix, matrix, (((0,), (0,)), ((), ())), preferred_element_type=jnp.float32
    )


def newton_steps(matrix):
    for iteration in range(ITERS):
        product = gram_product(matrix)
        gram_matrix = product.astype(jnp.bfloat16)
        squared = jnp.dot(gram_matrix, gram_matrix, preferred_element_type=jnp.float32)
        polynomial = (coef_b * gram_matrix.astype(jnp.float32) + coef_c * squared).astype(
            jnp.bfloat16
        )
        mixed = jnp.dot(matrix, polynomial, preferred_element_type=jnp.float32)
        matrix = (coef_a * matrix.astype(jnp.float32) + mixed).astype(jnp.bfloat16)
    return matrix


def per_device(grads, momentum):
    pods = lax.axis_size("outer")
    pod_index = lax.axis_index("outer")
    devices = lax.axis_size("dp")
    dp_index = lax.axis_index("dp")
    local = grads[0]
    count = local.shape[0]
    per_pod = count // pods
    rows = local.shape[1]
    width = local.shape[2]
    height = rows * devices
    update_scale = 0.2 * math.sqrt(max(height, width))
    summed = lax.psum(local, "outer")
    momentum_new = momentum_rate * momentum + summed
    steering_all = summed + momentum_rate * momentum_new
    steering = lax.dynamic_slice_in_dim(steering_all, pod_index * per_pod, per_pod, 0)
    steering = steering.astype(jnp.bfloat16)
    stride = max(devices // count, 1)
    piece = steering[0]
    whole = lax.all_gather(piece, "dp", axis=0, tiled=True)
    values = whole.astype(jnp.float32)
    norm_value = jnp.sqrt(jnp.sum(values * values))
    start = (values / (norm_value + epsilon)).astype(jnp.bfloat16)
    owner_index = (pod_index * per_pod + 0) * stride % devices
    finished = lax.cond(
        dp_index == owner_index, lambda: newton_steps(start), lambda: jnp.zeros_like(start)
    )
    finished = broadcast(finished, "dp", owner_index)
    results = [lax.dynamic_slice_in_dim(finished, dp_index * rows, rows, 0)]
    mine = jnp.stack(results)
    gathered = lax.all_gather(mine, "outer", axis=0, tiled=True)
    return (momentum_new, update_scale * gathered.astype(jnp.float32))


def solution(mesh):
    in_specs = (P("outer", None, "dp", None), P(None, "dp", None))
    out_specs = (P(None, "dp", None), P(None, "dp", None))
    return jax.shard_map(
        per_device, mesh=mesh, in_specs=in_specs, out_specs=out_specs, check_vma=False
    )
```

profile of v0, /device:TPU:1, one launch (start us, length us, event | category | flops | bytes accessed | tf_op | source)
XLA Modules:
  0.0 2071.7 jit_solution(10774868268015892276)
XLA Ops:
  7.2 0.0 all-reduce.3.cloned.1.call-start
  7.2 0.7 all-reduce.3.cloned.1.call-update
  7.9 0.0 all-gather.4.cloned.1.call-start
  8.0 94.5 %all-reduce.3.cloned.1.call-done = f32[6,8,576]{2,1,0:T(8,128)} async-done(((f32[6,8,576]{2,1,0:T(8,128)}), f32[6,8,576]{2,1,0:T(8,128)}) %all-reduce.3.cloned.1.call-update) | async-done | bytes 110608 | tf_op jit(solution)/shard_map/psum | solution.py:54
  102.5 1.0 multiply_add_fusion
  103.5 0.0 copy-start.1
  103.5 1.4 fusion.12
  104.9 0.0 all-gather.4.cloned.1.call-update
  104.9 0.0 all-reduce.5.cloned.1.call-start
  104.9 142.5 %all-gather.4.cloned.1.call-done = bf16[1,1024,576]{2,1,0:T(8,128)(2,1)} async-done(((bf16[1,8,576]{2,1,0:T(8,128)(2,1)}), bf16[1,1024,576]{2,1,0:T(8,128)(2,1)}) %all-gather.4.cloned.1.call-update) | async-done | bytes 1179664 | tf_op jit(solution)/shard_map/all_gather | solution.py:61
  247.5 0.0 copy-start
  247.5 2.7 fusion.10
  250.9 0.0 copy-done
  250.9 0.3 fusion.11
  251.1 0.0 copy-done.1
  251.2 0.1 conditional.1
  251.2 0.1 broadcast.11.clone
  251.3 1.2 broadcast_select_fusion
  252.5 0.0 all-reduce.5.cloned.1.call-update
  252.5 1786.8 %all-reduce.5.cloned.1.call-done = bf16[1024,576]{1,0:T(8,128)(2,1)} async-done(((bf16[1024,576]{1,0:T(8,128)(2,1)}), bf16[1024,576]{1,0:T(8,128)(2,1)}) %all-reduce.5.cloned.1.call-update) | async-done | bytes 1179664 | tf_op jit(solution)/shard_map/psum | solution.py:20
  2039.3 0.7 constant_dynamic-slice_fusion
  2040.0 24.5 %all-gather.1 = bf16[48,576]{1,0:T(8,128)(2,1)S(1)} all-gather(bf16[8,576]{1,0:T(8,128)(2,1)S(1)} %constant_dynamic-slice_fusion), channel_id=3, replica_groups=mesh['outer'=6,'dp'=128] {'outer'}, dimensions={0}, use_global_device_ids=true | all-gather | bytes 64512 | tf_op jit(solution)/shard_map/all_gather | solution.py:72
  2064.5 0.7 multiply_bitcast_fusion
Async XLA Ops:
  7.2 95.3 %all-reduce.3.cloned.1.call-start = ((), (), s32[]{:S(2)}) async-start(), calls=%async_computation | async-start | bytes 245760 | tf_op jit(solution)/shard_map/psum | solution.py:54
  7.9 239.6 %all-gather.4.cloned.1.call-start = ((), (), s32[]{:S(2)}) async-start(), calls=%async_computation.2 | async-start | bytes 1320960 | tf_op jit(solution)/shard_map/all_gather | solution.py:61
  103.5 147.7 %copy-start.1 = (f32[6,8,576]{2,1,0:T(8,128)}, f32[6,8,576]{2,1,0:T(8,128)S(1)}, u32[]{:S(2)}) copy-start(f32[6,8,576]{2,1,0:T(8,128)S(1)} %multiply_add_fusion) | copy-start | bytes 331780
  104.9 1934.5 %all-reduce.5.cloned.1.call-start = ((), (), s32[]{:S(2)}) async-start(), calls=%async_computation.1 | async-start | bytes 2621440 | tf_op jit(solution)/shard_map/psum | solution.py:20
  247.5 3.4 copy-start
Sparse Core Ops, SparseCore 0:
  11.2 91.2 all-reduce.2
  109.4 138.0 all-gather.3
  252.6 1786.6 all-reduce.4
where the time goes:
time: 2080 us; the launch traced here: 2070 us
  waiting for transfers between devices  2020 us (97%)
  blocking collectives  24.5 us (1%)
    psum x1, waiting for transfers between devices, broadcast(): return lax.psum(kept, axis)  1790 us
    all_gather x1, waiting for transfers between devices, per_device(): whole = lax.all_gather(piece, 'dp', axis=0, tiled=True)  143 us
    psum x1, waiting for transfers between devices, per_device(): summed = lax.psum(local, 'outer')  94.5 us
  transfers between devices with their start and end apart: 3, of which 3 were waited for; matrix products, arithmetic and copies ran while one was open for 0% of the time, Pallas kernels for 0%

commit v1 on v0

v1 whole, which is shorter than its diff:
```python
import functools
import math

import jax
import jax.numpy as jnp
from jax import lax
from jax.experimental import pallas as pl
from jax.experimental.pallas import tpu as pltpu
from jax.sharding import PartitionSpec as P

MESH = pl.DeviceIdType.MESH

coef_a = 3.4445
coef_b = -4.775
coef_c = 2.0315
momentum_rate = 0.95
epsilon = 1e-06

PODS = 6
NX = 4
NY = 8
CORES = 2
LANES = 128


def dot(left, right):
    return jnp.dot(left, right, preferred_element_type=jnp.float32)


def gram_product(matrix):
    return lax.dot_general(
        matrix, matrix, (((0,), (0,)), ((), ())), preferred_element_type=jnp.float32
    )


def kernel(
    scale,
    grads,
    momentum,
    momentum_out,
    update_out,
    own_grad,
    own_momentum,
    parts,
    moments,
    block,
    mirror_block,
    rows,
    finals,
    result,
    local_sem,
    part_send,
    part_recv,
    moment_send,
    moment_recv,
    mirror_send,
    mirror_recv,
    y_send,
    y_recv,
    x_send,
    x_recv,
    core_send,
    core_recv,
    final_send,
    final_recv,
):
    width = grads.shape[-1]
    wide = rows.shape[-1]
    pod = lax.axis_index("outer")
    dp = lax.axis_index("dp")
    core = lax.rem(dp, 2)
    y = lax.rem(dp // 2, NY)
    half = lax.rem(dp // (2 * NY), 2)
    x = dp // (4 * NY)

    def dp_of(x_, half_, y_, core_):
        return ((x_ * 2 + half_) * NY + y_) * 2 + core_

    def matrix_of(pod_):
        return pod_ + half * (PODS - 1 - 2 * pod_)

    mine = matrix_of(pod)
    pods = [lax.rem(pod + d, PODS) for d in range(1, PODS)]
    mirror = (PODS - 1 - pod, dp_of(x, 1 - half, y, core))
    along_y = [(pod, dp_of(x, half, lax.rem(y + k, NY), core)) for k in range(1, NY)]
    along_x = [(pod, dp_of(lax.rem(x + k, NX), half, y, core)) for k in range(1, NX)]
    sibling = (pod, dp_of(x, half, y, 1 - core))

    load_grad = pltpu.make_async_copy(grads.at[0, mine], own_grad, local_sem.at[0])
    load_momentum = pltpu.make_async_copy(momentum.at[mine], own_momentum, local_sem.at[1])
    load_grad.start()
    load_momentum.start()

    barrier = pltpu.get_barrier_semaphore()
    peers = [(p, dp) for p in pods] + [mirror] + along_y + along_x + [sibling]
    for peer in peers:
        pl.semaphore_signal(barrier, inc=1, device_id=peer, device_id_type=MESH)
    pl.semaphore_wait(barrier, len(peers))

    def remote(source, target, send_sem, recv_sem, device):
        return pltpu.make_async_remote_copy(
            src_ref=source,
            dst_ref=target,
            send_sem=send_sem,
            recv_sem=recv_sem,
            device_id=device,
            device_id_type=MESH,
        )

    sent = []
    for d, p in enumerate(pods):
        copy = remote(
            grads.at[0, matrix_of(p)], parts.at[d], part_send.at[d], part_recv.at[d], (p, dp)
        )
        copy.start()
        sent.append(copy)
    block[...] = jnp.zeros_like(block)
    load_grad.wait()
    load_momentum.wait()
    summed = own_grad[...]
    for d, copy in enumerate(sent):
        copy.wait_recv()
        summed = summed + parts[d]
    momentum_new = momentum_rate * own_momentum[...] + summed
    steering = summed + momentum_rate * momentum_new
    block[:, :width] = steering.astype(jnp.bfloat16)

    to_mirror = remote(block, mirror_block, mirror_send, mirror_recv, mirror)
    to_mirror.start()
    sent.append(to_mirror)
    moments[mine] = momentum_new
    to_mirror.wait_recv()
    pair = jnp.concatenate(
        [block[...].astype(jnp.float32), mirror_block[...].astype(jnp.float32)], axis=0
    )
    rows[core, x, y] = pair.astype(jnp.bfloat16)

    to_y = []
    for k, peer in enumerate(along_y):
        here = rows.at[core, x, y]
        copy = remote(here, here, y_send.at[k], y_recv.at[k], peer)
        copy.start()
        to_y.append(copy)
    to_pods = []
    for d, p in enumerate(pods):
        here = moments.at[mine]
        copy = remote(here, here, moment_send.at[d], moment_recv.at[d], (p, dp))
        copy.start()
        to_pods.append(copy)
    for copy in to_y:
        copy.wait_recv()

    to_x = []
    here = rows.at[core, x]
    for k, peer in enumerate(along_x):
        copy = remote(here, here, x_send.at[k], x_recv.at[k], peer)
        copy.start()
        to_x.append(copy)
    to_core = [remote(here, here, core_send.at[0], core_recv.at[0], sibling)]
    to_core[0].start()
    for k in range(1, NX):
        to_x[k - 1].wait_recv()
        there = rows.at[core, lax.rem(x - k + NX, NX)]
        copy = remote(there, there, core_send.at[k], core_recv.at[k], sibling)
        copy.start()
        to_core.append(copy)
    for copy in to_core:
        copy.wait_recv()

    raw = gram_product(rows[...].reshape(-1, wide))
    down = lax.broadcasted_iota(jnp.int32, (wide, wide), 0)
    across = lax.broadcasted_iota(jnp.int32, (wide, wide), 1)
    trace = jnp.sum(jnp.where(down == across, raw, 0.0), keepdims=True)
    inverse = 1.0 / (jnp.sqrt(trace) + epsilon)
    gram = (raw * (inverse * inverse)).astype(jnp.bfloat16)
    start = (pair * inverse).astype(jnp.bfloat16)
    polynomial = (coef_b * gram.astype(jnp.float32) + coef_c * dot(gram, gram)).astype(
        jnp.bfloat16
    )
    first = (coef_a * start.astype(jnp.float32) + dot(start, polynomial)).astype(jnp.bfloat16)
    half_way = (coef_a * gram.astype(jnp.float32) + dot(gram, polynomial)).astype(jnp.bfloat16)
    gram = (coef_a * half_way.astype(jnp.float32) + dot(polynomial, half_way)).astype(
        jnp.bfloat16
    )
    polynomial = (coef_b * gram.astype(jnp.float32) + coef_c * dot(gram, gram)).astype(
        jnp.bfloat16
    )
    second = coef_a * first.astype(jnp.float32) + dot(first, polynomial)
    finals[mine] = second[: block.shape[0]].astype(jnp.bfloat16)

    to_finals = []
    here = finals.at[mine]
    for d, p in enumerate(pods):
        copy = remote(here, here, final_send.at[d], final_recv.at[d], (p, dp))
        copy.start()
        to_finals.append(copy)
    for copy in to_pods:
        copy.wait_recv()
    store_moments = pltpu.make_async_copy(moments, momentum_out, local_sem.at[0])
    store_moments.start()
    for copy in to_finals:
        copy.wait_recv()
    result[...] = scale * finals[:, :, :width].astype(jnp.float32)
    store_update = pltpu.make_async_copy(result, update_out, local_sem.at[1])
    store_update.start()
    for copy in sent + to_y + to_pods + to_x + to_core + to_finals:
        copy.wait_send()
    store_moments.wait()
    store_update.wait()


def per_device(grads, momentum):
    _, count, depth, width = grads.shape
    wide = -(-width // LANES) * LANES
    height = depth * NX * 2 * NY * CORES
    scale = 0.2 * math.sqrt(max(height, width))
    half, single = jnp.bfloat16, jnp.float32
    dma = pltpu.SemaphoreType.DMA
    return pl.pallas_call(
        functools.partial(kernel, scale),
        out_shape=[jax.ShapeDtypeStruct(momentum.shape, single)] * 2,
        in_specs=[pl.BlockSpec(memory_space=pl.ANY)] * 2,
        out_specs=[pl.BlockSpec(memory_space=pl.ANY)] * 2,
        scratch_shapes=[
            pltpu.VMEM((depth, width), single),
            pltpu.VMEM((depth, width), single),
            pltpu.VMEM((PODS - 1, depth, width), single),
            pltpu.VMEM((count, depth, width), single),
            pltpu.VMEM((depth, wide), half),
            pltpu.VMEM((depth, wide), half),
            pltpu.VMEM((CORES, NX, NY, 2 * depth, wide), half),
            pltpu.VMEM((count, depth, wide), half),
            pltpu.VMEM((count, depth, width), single),
            dma((2,)),
            dma((PODS - 1,)),
            dma((PODS - 1,)),
            dma((PODS - 1,)),
            dma((PODS - 1,)),
            dma,
            dma,
            dma((NY - 1,)),
            dma((NY - 1,)),
            dma((NX - 1,)),
            dma((NX - 1,)),
            dma((NX,)),
            dma((NX,)),
            dma((PODS - 1,)),
            dma((PODS - 1,)),
        ],
        compiler_params=pltpu.CompilerParams(collective_id=0, has_side_effects=True),
    )(grads, momentum)


def solution(mesh):
    in_specs = (P("outer", None, "dp", None), P(None, "dp", None))
    out_specs = (P(None, "dp", None), P(None, "dp", None))
    return jax.shard_map(
        per_device, mesh=mesh, in_specs=in_specs, out_specs=out_specs, check_vma=False
    )
```

time: 2080 us -> 58 us (0.03)
  waiting for transfers between devices: 2020 us -> 0 us
  Pallas kernels: 0 us -> 54.9 us
  blocking collectives: 24.5 us -> 0 us
    psum x2 -> x0, waiting for transfers between devices: 1880 us -> none  [the longest x1 1790 us: broadcast(): return lax.psum(kept, axis)]
    all_gather x1 -> x0, waiting for transfers between devices: 143 us -> none  [per_device(): whole = lax.all_gather(piece, 'dp', axis=0, tiled=True)]
    pallas_call x0 -> x1, Pallas kernels: none -> 54.9 us  [per_device(): pl.pallas_call(functools.partial(kernel, scale), out_shape=[jax.ShapeDtyp...]
    all_gather x1 -> x0, blocking collectives: 24.5 us -> none  [per_device(): gathered = lax.all_gather(mine, 'outer', axis=0, tiled=True)]
  transfers between devices with their start and end apart: 3 -> 0, of which waited for: 3 -> 0; matrix products, arithmetic and copies ran while one was open for 0% -> 0% of each run, Pallas kernels for 0% -> 0%
where the time goes in v1:
time: 58 us; the launch traced here: 57.8 us
  Pallas kernels  54.9 us (95%)
  local copies, waits for them, and re-layouts  2.25 us (4%)
  between operations  0.65 us (1%)
    pallas_call x1, Pallas kernels, per_device(): pl.pallas_call(functools.partial(kernel, scale), out_shape=[jax.ShapeDtyp...  54.9 us
    unnamed x4, local copies, waits for them, and re-layouts  2.25 us

profile of v1, /device:TPU:1, one launch (start us, length us, event | category | flops | bytes accessed | tf_op | source)
XLA Modules:
  0.0 57.8 jit_solution(7880577760644050104)
XLA Ops:
  0.6 54.9 %shard_map.41 = (f32[6,8,576]{2,1,0:T(8,128)}, f32[6,8,576]{2,1,0:T(8,128)}) custom-call(f32[1,6,8,576]{3,2,1,0:T(8,128)} %grads.1, f32[6,8,576]{2,1,0:T(8,128)} %momentum.1), custom_call_target="tpu_custom_call" | custom-call | tf_op jit(solution)/shard_map/pallas_call | solution.py:219
  55.6 0.0 copy-start
  55.6 1.6 %copy.6 = f32[6,8,576]{2,1,0:T(8,128)} copy(f32[6,8,576]{2,1,0:T(8,128)} %get-tuple-element.4) | data formatting | bytes 221184
  57.2 0.0 copy-done
  57.2 0.6 %copy.7 = f32[6,8,576]{2,1,0:T(8,128)} copy(f32[6,8,576]{2,1,0:T(8,128)S(1)} %copy-done) | data formatting | bytes 221184
Async XLA Ops:
  55.6 1.6 %copy-start = (f32[6,8,576]{2,1,0:T(8,128)S(1)}, f32[6,8,576]{2,1,0:T(8,128)}, u32[]{:S(2)}) copy-start(f32[6,8,576]{2,1,0:T(8,128)} %get-tuple-element.5) | copy-start | bytes 331780

commit v2 on v0

v2 whole, which is shorter than its diff:
```python
import functools
import math

import jax
import jax.numpy as jnp
from jax import lax
from jax.experimental import pallas as pl
from jax.experimental.pallas import tpu as pltpu
from jax.sharding import PartitionSpec as P

MESH = pl.DeviceIdType.MESH

coef_a = 3.4445
coef_b = -4.775
coef_c = 2.0315
momentum_rate = 0.95
epsilon = 1e-06

PODS = 6
NZ = 12
NX = 4
NY = 8
CORES = 2
LANES = 128
ALONG_Y = (1, 7, 2, 6, 3, 5, 4)
ALONG_X = (1, 3, 2)
GROUPS = ((0, 1), (1, 3), (3, 5), (5, 8))
FAR_MATRICES = (3, 2, 4, 1, 5, 0)
FAR_CHIPS = (6, 5, 7, 4, 8, 3, 9, 2, 10, 1, 11, 0)


def dot(left, right):
    return jnp.dot(left, right, preferred_element_type=jnp.float32)


def gram_product(matrix):
    return lax.dot_general(
        matrix, matrix, (((0,), (0,)), ((), ())), preferred_element_type=jnp.float32
    )


def kernel(
    scale,
    grads,
    momentum,
    momentum_out,
    update_out,
    my_grads,
    my_momentum,
    terms,
    parts,
    sums,
    totals,
    rows,
    raw,
    pieces,
    finals,
    result,
    local_sem,
    term_send,
    term_recv,
    y_send,
    y_recv,
    x_send,
    x_recv,
    total_send,
    total_recv,
    final_send,
    final_recv,
):
    width = grads.shape[-1]
    wide = rows.shape[-1]
    pod = lax.axis_index("outer")
    dp = lax.axis_index("dp")
    core = lax.rem(dp, 2)
    y = lax.rem(dp // 2, NY)
    half = lax.rem(dp // (2 * NY), 2)
    x = dp // (4 * NY)
    z = half * PODS + pod
    near = z // 2
    holder = jnp.logical_and(core == 1, lax.rem(z, 2) == 0)

    def device(x_, y_, z_, core_):
        return (lax.rem(z_, PODS), ((x_ * 2 + z_ // PODS) * NY + y_) * 2 + core_)

    def remote(source, target, send_sem, recv_sem, peer):
        return pltpu.make_async_remote_copy(
            src_ref=source,
            dst_ref=target,
            send_sem=send_sem,
            recv_sem=recv_sem,
            device_id=peer,
            device_id_type=MESH,
        )

    load_grads = pltpu.make_async_copy(grads.at[0], my_grads, local_sem.at[0])
    load_momentum = pltpu.make_async_copy(momentum, my_momentum, local_sem.at[1])
    load_grads.start()
    load_momentum.start()

    along_y = [device(x, lax.rem(y + k, NY), z, 1) for k in ALONG_Y]
    along_x = [device(lax.rem(x + k, NX), y, z, 1) for k in ALONG_X]
    barrier = pltpu.get_barrier_semaphore()

    def greet(peer):
        pl.semaphore_signal(barrier, inc=1, device_id=peer, device_id_type=MESH)

    @pl.when(holder)
    def _():
        for d in FAR_CHIPS:
            for c in range(CORES):
                if (d, c) != (0, 1):
                    greet(device(x, y, lax.rem(z + d, NZ), c))
        for peer in along_y + along_x:
            greet(peer)

    @pl.when(jnp.logical_not(holder))
    def _():
        for s in FAR_MATRICES:
            greet(device(x, y, 2 * lax.rem(near + s, PODS), 1))

    load_grads.wait()
    load_momentum.wait()
    terms[...] = (1 + momentum_rate) * my_grads[...] + (
        momentum_rate * momentum_rate / PODS
    ) * my_momentum[...]

    @pl.when(holder)
    def _():
        pl.semaphore_wait(barrier, NZ * CORES - 1 + len(along_y) + len(along_x))

    @pl.when(jnp.logical_not(holder))
    def _():
        pl.semaphore_wait(barrier, PODS)

    def term_copy(s):
        j = lax.rem(near + s, PODS)
        return remote(
            terms.at[j],
            parts.at[z, core],
            term_send.at[s],
            term_recv.at[z, core],
            device(x, y, 2 * j, 1),
        )

    for s in FAR_MATRICES:
        if s:
            term_copy(s).start()

    @pl.when(jnp.logical_not(holder))
    def _():
        term_copy(0).start()

    @pl.when(holder)
    def _():
        parts[z, 1] = terms[near]
        rows[0, 0] = jnp.zeros_like(rows[0, 0])
        for z_ in range(NZ):
            for c in range(CORES):
                arrived = remote(
                    terms.at[0],
                    parts.at[z_, c],
                    term_send.at[0],
                    term_recv.at[z_, c],
                    device(x, y, z, 0),
                )
                if c == 1 and z_ % 2 == 0:
                    pl.when(z_ != z)(arrived.wait_recv)
                else:
                    arrived.wait_recv()
        for h in range(2):
            total = parts[h * PODS]
            for k in range(1, PODS):
                total = total + parts[h * PODS + k]
            sums[pl.ds(h * CORES, CORES)] = total
        steering = sums[...].reshape(-1, width).astype(jnp.bfloat16)
        rows[0, 0, :, :width] = steering

        to_y = []
        for i, peer in enumerate(along_y):
            copy = remote(rows.at[0, 0], rows.at[0, i + 1], y_send.at[i], y_recv.at[i], peer)
            copy.start()
            to_y.append(copy)
        to_x = [[] for _ in along_x]
        for g, (low, high) in enumerate(GROUPS):
            for i in range(max(low, 1), high):
                to_y[i - 1].wait_recv()
            for i, peer in enumerate(along_x):
                copy = remote(
                    rows.at[0, pl.ds(low, high - low)],
                    rows.at[i + 1, pl.ds(low, high - low)],
                    x_send.at[i, g],
                    x_recv.at[i, g],
                    peer,
                )
                copy.start()
                to_x[i].append(copy)

        def total_copy(d, c):
            z_ = lax.rem(z + d, NZ)
            return remote(
                sums.at[(z_ // PODS) * CORES + c],
                totals.at[near],
                total_send.at[d, c],
                total_recv.at[near],
                device(x, y, z_, c),
            )

        for d in FAR_CHIPS:
            for c in range(CORES):
                if (d, c) != (0, 1):
                    total_copy(d, c).start()
        totals[near] = sums[half * CORES + 1]

        raw[...] = gram_product(rows[0].reshape(-1, wide))
        for i in range(len(along_x)):
            for copy in to_x[i]:
                copy.wait_recv()
            raw[...] += gram_product(rows[i + 1].reshape(-1, wide))

        down = lax.broadcasted_iota(jnp.int32, (wide, wide), 0)
        across = lax.broadcasted_iota(jnp.int32, (wide, wide), 1)
        trace = jnp.sum(jnp.where(down == across, raw[...], 0.0), keepdims=True)
        inverse = 1.0 / (jnp.sqrt(trace) + epsilon)
        gram = (raw[...] * (inverse * inverse)).astype(jnp.bfloat16)
        start = (rows[0, 0].astype(jnp.float32) * inverse).astype(jnp.bfloat16)
        polynomial = (
            coef_b * gram.astype(jnp.float32) + coef_c * dot(gram, gram)
        ).astype(jnp.bfloat16)
        first = (coef_a * start.astype(jnp.float32) + dot(start, polynomial)).astype(
            jnp.bfloat16
        )
        half_way = (coef_a * gram.astype(jnp.float32) + dot(gram, polynomial)).astype(
            jnp.bfloat16
        )
        gram = (coef_a * half_way.astype(jnp.float32) + dot(polynomial, half_way)).astype(
            jnp.bfloat16
        )
        polynomial = (
            coef_b * gram.astype(jnp.float32) + coef_c * dot(gram, gram)
        ).astype(jnp.bfloat16)
        second = coef_a * first.astype(jnp.float32) + dot(first, polynomial)
        depth = pieces.shape[1]
        for q in range(2 * CORES):
            pieces[q] = second[q * depth : (q + 1) * depth].astype(jnp.bfloat16)

        def final_copy(d, c):
            z_ = lax.rem(z + d, NZ)
            return remote(
                pieces.at[(z_ // PODS) * CORES + c],
                finals.at[near],
                final_send.at[d, c],
                final_recv.at[near],
                device(x, y, z_, c),
            )

        for d in FAR_CHIPS:
            for c in range(CORES):
                if (d, c) != (0, 1):
                    final_copy(d, c).start()
        finals[near] = pieces[half * CORES + 1]
        for copy in to_y + sum(to_x, []):
            copy.wait_send()
        for d in FAR_CHIPS:
            for c in range(CORES):
                if (d, c) != (0, 1):
                    total_copy(d, c).wait_send()
                    final_copy(d, c).wait_send()

    def await_matrices(buffer, sem):
        for j in range(PODS):
            arrived = remote(
                buffer.at[j], buffer.at[j], term_send.at[0], sem.at[j], device(x, y, z, 1 - core)
            )
            pl.when(jnp.logical_not(jnp.logical_and(holder, near == j)))(arrived.wait_recv)

    await_matrices(totals, total_recv)
    my_momentum[...] = (1 / (1 + momentum_rate)) * totals[...] + (
        momentum_rate - momentum_rate * momentum_rate / (1 + momentum_rate)
    ) * my_momentum[...]
    store_momentum = pltpu.make_async_copy(my_momentum, momentum_out, local_sem.at[0])
    store_momentum.start()
    await_matrices(finals, final_recv)
    result[...] = scale * finals[:, :, :width].astype(jnp.float32)
    store_update = pltpu.make_async_copy(result, update_out, local_sem.at[1])
    store_update.start()
    for s in FAR_MATRICES:
        if s:
            term_copy(s).wait_send()

    @pl.when(jnp.logical_not(holder))
    def _():
        term_copy(0).wait_send()

    store_momentum.wait()
    store_update.wait()


def per_device(grads, momentum):
    _, count, depth, width = grads.shape
    wide = -(-width // LANES) * LANES
    height = depth * NX * 2 * NY * CORES
    scale = 0.2 * math.sqrt(max(height, width))
    half, single = jnp.bfloat16, jnp.float32
    dma = pltpu.SemaphoreType.DMA
    return pl.pallas_call(
        functools.partial(kernel, scale),
        out_shape=[jax.ShapeDtypeStruct(momentum.shape, single)] * 2,
        in_specs=[pl.BlockSpec(memory_space=pl.ANY)] * 2,
        out_specs=[pl.BlockSpec(memory_space=pl.ANY)] * 2,
        scratch_shapes=[
            pltpu.VMEM((count, depth, width), single),
            pltpu.VMEM((count, depth, width), single),
            pltpu.VMEM((count, depth, width), single),
            pltpu.VMEM((NZ, CORES, depth, width), single),
            pltpu.VMEM((2 * CORES, depth, width), single),
            pltpu.VMEM((count, depth, width), single),
            pltpu.VMEM((NX, NY, 2 * CORES * depth, wide), half),
            pltpu.VMEM((wide, wide), single),
            pltpu.VMEM((2 * CORES, depth, wide), half),
            pltpu.VMEM((count, depth, wide), half),
            pltpu.VMEM((count, depth, width), single),
            dma((2,)),
            dma((PODS,)),
            dma((NZ, CORES)),
            dma((NY - 1,)),
            dma((NY - 1,)),
            dma((NX - 1, len(GROUPS))),
            dma((NX - 1, len(GROUPS))),
            dma((NZ, CORES)),
            dma((PODS,)),
            dma((NZ, CORES)),
            dma((PODS,)),
        ],
        compiler_params=pltpu.CompilerParams(collective_id=0, has_side_effects=True),
    )(grads, momentum)


def solution(mesh):
    in_specs = (P("outer", None, "dp", None), P(None, "dp", None))
    out_specs = (P(None, "dp", None), P(None, "dp", None))
    return jax.shard_map(
        per_device, mesh=mesh, in_specs=in_specs, out_specs=out_specs, check_vma=False
    )
```

time: 2080 us -> 55 us (0.03)
  waiting for transfers between devices: 2020 us -> 0 us
  Pallas kernels: 0 us -> 52 us
  blocking collectives: 24.5 us -> 0 us
    psum x2 -> x0, waiting for transfers between devices: 1880 us -> none  [the longest x1 1790 us: broadcast(): return lax.psum(kept, axis)]
    all_gather x1 -> x0, waiting for transfers between devices: 143 us -> none  [per_device(): whole = lax.all_gather(piece, 'dp', axis=0, tiled=True)]
    pallas_call x0 -> x1, Pallas kernels: none -> 52 us  [per_device(): pl.pallas_call(functools.partial(kernel, scale), out_shape=[jax.ShapeDtyp...]
    all_gather x1 -> x0, blocking collectives: 24.5 us -> none  [per_device(): gathered = lax.all_gather(mine, 'outer', axis=0, tiled=True)]
  transfers between devices with their start and end apart: 3 -> 0, of which waited for: 3 -> 0; matrix products, arithmetic and copies ran while one was open for 0% -> 0% of each run, Pallas kernels for 0% -> 0%
where the time goes in v2:
time: 55 us; the launch traced here: 54.9 us
  Pallas kernels  52 us (95%)
  local copies, waits for them, and re-layouts  2.25 us (4%)
  between operations  0.65 us (1%)
    pallas_call x1, Pallas kernels, per_device(): pl.pallas_call(functools.partial(kernel, scale), out_shape=[jax.ShapeDtyp...  52 us
    unnamed x4, local copies, waits for them, and re-layouts  2.25 us

profile of v2, /device:TPU:1, one launch (start us, length us, event | category | flops | bytes accessed | tf_op | source)
XLA Modules:
  0.0 54.9 jit_solution(7206614526270593535)
XLA Ops:
  0.6 52.0 %shard_map.41 = (f32[6,8,576]{2,1,0:T(8,128)}, f32[6,8,576]{2,1,0:T(8,128)}) custom-call(f32[1,6,8,576]{3,2,1,0:T(8,128)} %grads.1, f32[6,8,576]{2,1,0:T(8,128)} %momentum.1), custom_call_target="tpu_custom_call" | custom-call | tf_op jit(solution)/shard_map/pallas_call | solution.py:306
  52.6 0.0 copy-start
  52.6 1.6 %copy.6 = f32[6,8,576]{2,1,0:T(8,128)} copy(f32[6,8,576]{2,1,0:T(8,128)} %get-tuple-element.4) | data formatting | bytes 221184
  54.2 0.0 copy-done
  54.2 0.6 %copy.7 = f32[6,8,576]{2,1,0:T(8,128)} copy(f32[6,8,576]{2,1,0:T(8,128)S(1)} %copy-done) | data formatting | bytes 221184
Async XLA Ops:
  52.6 1.6 %copy-start = (f32[6,8,576]{2,1,0:T(8,128)S(1)}, f32[6,8,576]{2,1,0:T(8,128)}, u32[]{:S(2)}) copy-start(f32[6,8,576]{2,1,0:T(8,128)} %get-tuple-element.5) | copy-start | bytes 331780

commit v3 on v2

v3 whole, which is shorter than its diff:
```python
import functools
import math

import jax
import jax.numpy as jnp
from jax import lax
from jax.experimental import pallas as pl
from jax.experimental.pallas import tpu as pltpu
from jax.sharding import PartitionSpec as P

MESH = pl.DeviceIdType.MESH

coef_a = 3.4445
coef_b = -4.775
coef_c = 2.0315
momentum_rate = 0.95
epsilon = 1e-06

PODS = 6
NZ = 12
NX = 4
NY = 8
CORES = 2
LANES = 128
HOLDERS = (0, 2, 4, 6, 8, 10)
VMEM_LIMIT = 24 << 20
ALONG_Y = (4, 3, 5, 2, 6, 1, 7)
ALONG_X = (1, 3, 2)
GROUPS = ((0, 4), (4, 6), (6, 8))
FAR_MATRICES = (3, 2, 4, 1, 5, 0)


def hold(j):
    if isinstance(j, int):
        return HOLDERS[j]
    return sum(jnp.where(j == k, HOLDERS[k], 0) for k in range(PODS))


def slot(y):
    return jnp.where(y < NY // 2, y, 3 * NY // 2 - 1 - y)


def dot(left, right):
    return jnp.dot(left, right, preferred_element_type=jnp.float32)


def gram_product(matrix):
    return lax.dot_general(
        matrix, matrix, (((0,), (0,)), ((), ())), preferred_element_type=jnp.float32
    )


def kernel(
    grads,
    momentum,
    totals,
    finals,
    my_grads,
    my_momentum,
    terms,
    parts,
    sums,
    rows,
    raw,
    pieces,
    local_sem,
    term_send,
    term_recv,
    y_send,
    y_recv,
    x_send,
    x_recv,
    total_send,
    total_recv,
    final_send,
    final_recv,
):
    width = grads.shape[-1]
    wide = rows.shape[-1]
    pod = lax.axis_index("outer")
    dp = lax.axis_index("dp")
    core = lax.rem(dp, 2)
    y = lax.rem(dp // 2, NY)
    half = lax.rem(dp // (2 * NY), 2)
    x = dp // (4 * NY)
    z = half * PODS + pod
    near = sum(jnp.where(z == HOLDERS[k], k, 0) for k in range(PODS))
    holder = jnp.logical_and(core == 1, hold(near) == z)
    near = jnp.where(hold(near) == z, near, z // 2)
    place = slot(y)

    def device(x_, y_, z_, core_):
        return (lax.rem(z_, PODS), ((x_ * 2 + z_ // PODS) * NY + y_) * 2 + core_)

    def remote(source, target, send_sem, recv_sem, peer):
        return pltpu.make_async_remote_copy(
            src_ref=source,
            dst_ref=target,
            send_sem=send_sem,
            recv_sem=recv_sem,
            device_id=peer,
            device_id_type=MESH,
        )

    def for_line(act):
        for z_ in range(NZ):
            for c in range(CORES):
                if c == 1 and z_ in [hold(j) for j in range(PODS)]:
                    pl.when(z_ != z)(functools.partial(act, z_, c))
                else:
                    act(z_, c)

    load_grads = pltpu.make_async_copy(grads.at[0], my_grads, local_sem.at[0])
    load_momentum = pltpu.make_async_copy(momentum, my_momentum, local_sem.at[1])
    load_grads.start()
    load_momentum.start()

    along_y = [device(x, lax.rem(y + k, NY), z, 1) for k in ALONG_Y]
    along_x = [device(lax.rem(x + k, NX), y, z, 1) for k in ALONG_X]
    barrier = pltpu.get_barrier_semaphore()

    def greet(peer):
        pl.semaphore_signal(barrier, inc=1, device_id=peer, device_id_type=MESH)

    @pl.when(holder)
    def _():
        for d in range(NZ):
            for c in range(CORES):
                if (d, c) != (0, 1):
                    greet(device(x, y, lax.rem(z + d, NZ), c))
        for peer in along_y + along_x:
            greet(peer)

    @pl.when(jnp.logical_not(holder))
    def _():
        for s in FAR_MATRICES:
            greet(device(x, y, hold(lax.rem(near + s, PODS)), 1))

    load_grads.wait()
    load_momentum.wait()
    terms[...] = (1 + momentum_rate) * my_grads[...] + (
        momentum_rate * momentum_rate / PODS
    ) * my_momentum[...]

    @pl.when(holder)
    def _():
        pl.semaphore_wait(barrier, NZ * CORES - 1 + len(along_y) + len(along_x))

    @pl.when(jnp.logical_not(holder))
    def _():
        pl.semaphore_wait(barrier, PODS)

    def term_copy(s):
        j = lax.rem(near + s, PODS)
        return remote(
            terms.at[j],
            parts.at[z, core],
            term_send.at[s],
            term_recv.at[z, core],
            device(x, y, hold(j), 1),
        )

    for s in FAR_MATRICES:
        if s:
            term_copy(s).start()

    @pl.when(jnp.logical_not(holder))
    def _():
        term_copy(0).start()

    @pl.when(holder)
    def _():
        parts[z, 1] = terms[near]
        rows[0, place] = jnp.zeros_like(rows[0, 0])
        for z_ in range(NZ):
            for c in range(CORES):
                arrived = remote(
                    terms.at[0],
                    parts.at[z_, c],
                    term_send.at[0],
                    term_recv.at[z_, c],
                    device(x, y, z, 0),
                )
                if c == 1 and z_ in [hold(j) for j in range(PODS)]:
                    pl.when(z_ != z)(arrived.wait_recv)
                else:
                    arrived.wait_recv()
        for h in range(2):
            total = parts[h * PODS]
            for k in range(1, PODS):
                total = total + parts[h * PODS + k]
            sums[pl.ds(h * CORES, CORES)] = total
        steering = sums[...].reshape(-1, width).astype(jnp.bfloat16)
        rows[0, place, :, :width] = steering

        to_y = []
        for i, peer in enumerate(along_y):
            mine = rows.at[0, place]
            copy = remote(mine, mine, y_send.at[i], y_recv.at[place], peer)
            copy.start()
            to_y.append(copy)
        to_x = [[] for _ in along_x]
        for g, (low, high) in enumerate(GROUPS):
            for i in range(low, high):
                other = rows.at[0, i]
                arrived = remote(other, other, y_send.at[0], y_recv.at[i], along_y[0])
                pl.when(i != place)(arrived.wait_recv)
            for i, peer in enumerate(along_x):
                copy = remote(
                    rows.at[0, pl.ds(low, high - low)],
                    rows.at[i + 1, pl.ds(low, high - low)],
                    x_send.at[i, g],
                    x_recv.at[i, g],
                    peer,
                )
                copy.start()
                to_x[i].append(copy)

        def total_copy(z_, c):
            return remote(
                sums.at[(z_ // PODS) * CORES + c],
                totals.at[near],
                total_send.at[z_, c],
                total_recv.at[near],
                device(x, y, z_, c),
            )

        for_line(lambda z_, c: total_copy(z_, c).start())
        totals[near] = sums[half * CORES + 1]

        raw[...] = gram_product(rows[0].reshape(-1, wide))
        for i in range(len(along_x)):
            for copy in to_x[i]:
                copy.wait_recv()
            raw[...] += gram_product(rows[i + 1].reshape(-1, wide))

        down = lax.broadcasted_iota(jnp.int32, (LANES, LANES), 0)
        across = lax.broadcasted_iota(jnp.int32, (LANES, LANES), 1)
        diagonal = raw[:LANES, :LANES]
        for i in range(LANES, wide, LANES):
            diagonal = diagonal + raw[i : i + LANES, i : i + LANES]
        trace = jnp.sum(jnp.where(down == across, diagonal, 0.0), keepdims=True)
        inverse = 1.0 / (jnp.sqrt(trace) + epsilon)
        gram = (raw[...] * (inverse * inverse)).astype(jnp.bfloat16)
        start = (rows[0, place].astype(jnp.float32) * inverse).astype(jnp.bfloat16)
        polynomial = (
            coef_b * gram.astype(jnp.float32) + coef_c * dot(gram, gram)
        ).astype(jnp.bfloat16)

        def step(value):
            return coef_a * value + dot(value.astype(jnp.bfloat16), polynomial)

        def next_gram(value):
            return step(dot(step(value).astype(jnp.bfloat16), gram))

        first = step(start.astype(jnp.float32)).astype(jnp.bfloat16).astype(jnp.float32)
        once = next_gram(first)
        second = coef_a * first + coef_b * once + coef_c * next_gram(once)
        depth = pieces.shape[1]
        for q in range(2 * CORES):
            pieces[q] = second[q * depth : (q + 1) * depth].astype(jnp.bfloat16)

        def final_copy(z_, c):
            return remote(
                pieces.at[(z_ // PODS) * CORES + c],
                finals.at[near],
                final_send.at[z_, c],
                final_recv.at[near],
                device(x, y, z_, c),
            )

        for_line(lambda z_, c: final_copy(z_, c).start())
        finals[near] = pieces[half * CORES + 1]
        for copy in to_y + sum(to_x, []):
            copy.wait_send()
        for_line(lambda z_, c: total_copy(z_, c).wait_send())
        for_line(lambda z_, c: final_copy(z_, c).wait_send())

    def await_matrices(buffer, sem):
        for j in range(PODS):
            arrived = remote(
                buffer.at[j], buffer.at[j], term_send.at[0], sem.at[j], device(x, y, z, 1 - core)
            )
            pl.when(jnp.logical_not(jnp.logical_and(holder, near == j)))(arrived.wait_recv)

    await_matrices(totals, total_recv)
    await_matrices(finals, final_recv)
    for s in FAR_MATRICES:
        if s:
            term_copy(s).wait_send()

    @pl.when(jnp.logical_not(holder))
    def _():
        term_copy(0).wait_send()


def per_device(grads, momentum):
    _, count, depth, width = grads.shape
    wide = -(-width // LANES) * LANES
    height = depth * NX * 2 * NY * CORES
    scale = 0.2 * math.sqrt(max(height, width))
    half, single = jnp.bfloat16, jnp.float32
    dma = pltpu.SemaphoreType.DMA
    totals, finals = pl.pallas_call(
        kernel,
        out_shape=[
            jax.ShapeDtypeStruct(momentum.shape, single),
            jax.ShapeDtypeStruct((count, depth, wide), half),
        ],
        in_specs=[pl.BlockSpec(memory_space=pltpu.HBM)] * 2,
        out_specs=[pl.BlockSpec(memory_space=pltpu.VMEM)] * 2,
        scratch_shapes=[
            pltpu.VMEM((count, depth, width), single),
            pltpu.VMEM((count, depth, width), single),
            pltpu.VMEM((count, depth, width), single),
            pltpu.VMEM((NZ, CORES, depth, width), single),
            pltpu.VMEM((2 * CORES, depth, width), single),
            pltpu.VMEM((NX, NY, 2 * CORES * depth, wide), half),
            pltpu.VMEM((wide, wide), single),
            pltpu.VMEM((2 * CORES, depth, wide), half),
            dma((2,)),
            dma((PODS,)),
            dma((NZ, CORES)),
            dma((NY - 1,)),
            dma((NY,)),
            dma((NX - 1, len(GROUPS))),
            dma((NX - 1, len(GROUPS))),
            dma((NZ, CORES)),
            dma((PODS,)),
            dma((NZ, CORES)),
            dma((PODS,)),
        ],
        compiler_params=pltpu.CompilerParams(
            collective_id=0, has_side_effects=True, vmem_limit_bytes=VMEM_LIMIT
        ),
    )(
        pltpu.with_memory_space_constraint(grads, pltpu.HBM),
        pltpu.with_memory_space_constraint(momentum, pltpu.HBM),
    )
    momentum_new = (1 / (1 + momentum_rate)) * totals + (
        momentum_rate - momentum_rate * momentum_rate / (1 + momentum_rate)
    ) * momentum
    return momentum_new, scale * finals[:, :, :width].astype(single)


def solution(mesh):
    in_specs = (P("outer", None, "dp", None), P(None, "dp", None))
    out_specs = (P(None, "dp", None), P(None, "dp", None))
    return jax.shard_map(
        per_device, mesh=mesh, in_specs=in_specs, out_specs=out_specs, check_vma=False
    )
```

time: 55 us -> 51.6 us (0.938)
  local copies, waits for them, and re-layouts: 2.25 us -> 0.01 us
  Pallas kernels: 52 us -> 50.1 us
  other arithmetic: 0 us -> 0.73 us
    unnamed x4 -> x2, local copies, waits for them, and re-layouts: 2.25 us -> 0.01 us
    pallas_call x1, Pallas kernels: 52 us -> 50.1 us  [per_device(): pl.pallas_call(kernel, out_shape=[jax.ShapeDtypeStruct(momentum.shape, si...]
    mul x0 -> x1, other arithmetic: none -> 0.73 us  [per_device(): return (momentum_new, scale * finals[:, :, :width].astype(single))]
where the time goes in v3:
time: 51.6 us; the launch traced here: 51.4 us
  Pallas kernels  50.1 us (97%)
  other arithmetic  0.73 us (1%)
  between operations  0.65 us (1%)
    pallas_call x1, Pallas kernels, per_device(): pl.pallas_call(kernel, out_shape=[jax.ShapeDtypeStruct(momentum.shape, si...  50.1 us

profile of v3, /device:TPU:1, one launch (start us, length us, event | category | flops | bytes accessed | tf_op | source)
XLA Modules:
  0.0 51.4 jit_solution(1083218284758421702)
XLA Ops:
  0.6 0.0 copy-start
  0.6 50.1 %shard_map.41 = (f32[6,8,576]{2,1,0:T(8,128)S(1)}, bf16[6,8,640]{2,1,0:T(8,128)(2,1)S(1)}) custom-call(f32[1,6,8,576]{3,2,1,0:T(8,128)} %grads.1, f32[6,8,576]{2,1,0:T(8,128)} %momentum.1), custom_call_target="tpu_custom_call" | custom-call | tf_op jit(solution)/shard_map/pallas_call | solution.py:304
  50.7 0.0 copy-done
  50.7 0.7 %convert_multiply_fusion = (f32[6,8,576]{2,1,0:T(8,128)}, f32[6,8,576]{2,1,0:T(8,128)}) fusion(bf16[6,8,640]{2,1,0:T(8,128)(2,1)S(1)} %get-tuple-element.5, f32[6,8,576]{2,1,0:T(8,128)S(1)} %copy-done, f32[6,8,576]{2,1,0:T(8,128)S(1)} %get-tuple-element.4), kind=kLoop, calls=%fused_computation | loop fusion | flops 138240 | bytes 497664 | tf_op jit(solution)/shard_map/mul | solution.py:343
Async XLA Ops:
  0.6 50.1 %copy-start = (f32[6,8,576]{2,1,0:T(8,128)S(1)}, f32[6,8,576]{2,1,0:T(8,128)}, u32[]{:S(2)}) copy-start(f32[6,8,576]{2,1,0:T(8,128)} %momentum.1) | copy-start | bytes 331780

commit v4 on v3

--- a/solution.py
+++ b/solution.py
@@ -22,11 +22,12 @@
 NY = 8
 CORES = 2
 LANES = 128
-HOLDERS = (0, 2, 4, 6, 8, 10)
+HOLDERS = (0, 2, 3, 5, 8, 10)
 VMEM_LIMIT = 24 << 20
 ALONG_Y = (4, 3, 5, 2, 6, 1, 7)
 ALONG_X = (1, 3, 2)
-GROUPS = ((0, 4), (4, 6), (6, 8))
+HANDED = {0: 0, 1: 1, 2: 0, 3: 1, 4: 0, 5: 1, 6: 0}
+LAG = 4
 FAR_MATRICES = (3, 2, 4, 1, 5, 0)
 
 
@@ -199,22 +200,33 @@
             copy = remote(mine, mine, y_send.at[i], y_recv.at[place], peer)
             copy.start()
             to_y.append(copy)
-        to_x = [[] for _ in along_x]
-        for g, (low, high) in enumerate(GROUPS):
-            for i in range(low, high):
-                other = rows.at[0, i]
-                arrived = remote(other, other, y_send.at[0], y_recv.at[i], along_y[0])
-                pl.when(i != place)(arrived.wait_recv)
-            for i, peer in enumerate(along_x):
-                copy = remote(
-                    rows.at[0, pl.ds(low, high - low)],
-                    rows.at[i + 1, pl.ds(low, high - low)],
-                    x_send.at[i, g],
-                    x_recv.at[i, g],
-                    peer,
-                )
-                copy.start()
-                to_x[i].append(copy)
+        def x_copy(i, b):
+            via = HANDED.get(b) if i == 2 else None
+            source = rows.at[0 if via is None else via + 1, b]
+            return remote(
+                source,
+                rows.at[i + 1, b],
+                x_send.at[i, b],
+                x_recv.at[i, b],
+                along_x[i if via is None else via],
+            )
+
+        def pass_on(b):
+            if b in HANDED:
+                x_copy(HANDED[b], b).wait_recv()
+                x_copy(2, b).start()
+
+        for b in range(NY):
+            other = rows.at[0, b]
+            arrived = remote(other, other, y_send.at[0], y_recv.at[b], along_y[0])
+            pl.when(b != place)(arrived.wait_recv)
+            x_copy(0, b).start()
+            x_copy(1, b).start()
+            if b not in HANDED:
+                x_copy(2, b).start()
+            pass_on(b - LAG)
+        for b in range(NY - LAG, NY):
+            pass_on(b)
 
         def total_copy(z_, c):
             return remote(
@@ -230,8 +242,9 @@
 
         raw[...] = gram_product(rows[0].reshape(-1, wide))
         for i in range(len(along_x)):
-            for copy in to_x[i]:
-                copy.wait_recv()
+            for b in range(NY):
+                if HANDED.get(b) != i:
+                    x_copy(i, b).wait_recv()
             raw[...] += gram_product(rows[i + 1].reshape(-1, wide))
 
         down = lax.broadcasted_iota(jnp.int32, (LANES, LANES), 0)
@@ -271,8 +284,11 @@
 
         for_line(lambda z_, c: final_copy(z_, c).start())
         finals[near] = pieces[half * CORES + 1]
-        for copy in to_y + sum(to_x, []):
+        for copy in to_y:
             copy.wait_send()
+        for i in range(len(along_x)):
+            for b in range(NY):
+                x_copy(i, b).wait_send()
         for_line(lambda z_, c: total_copy(z_, c).wait_send())
         for_line(lambda z_, c: final_copy(z_, c).wait_send())
 
@@ -323,8 +339,8 @@
             dma((NZ, CORES)),
             dma((NY - 1,)),
             dma((NY,)),
-            dma((NX - 1, len(GROUPS))),
-            dma((NX - 1, len(GROUPS))),
+            dma((NX - 1, NY)),
+            dma((NX - 1, NY)),
             dma((NZ, CORES)),
             dma((PODS,)),
             dma((NZ, CORES)),

time: 51.6 us -> 48.9 us (0.948)
  Pallas kernels: 50.1 us -> 47.4 us
    pallas_call x1, Pallas kernels: 50.1 us -> 47.4 us  [per_device(): pl.pallas_call(kernel, out_shape=[jax.ShapeDtypeStruct(momentum.shape, si...]
where the time goes in v4:
time: 48.9 us; the launch traced here: 48.7 us
  Pallas kernels  47.4 us (97%)
  other arithmetic  0.73 us (1%)
  between operations  0.65 us (1%)
    pallas_call x1, Pallas kernels, per_device(): pl.pallas_call(kernel, out_shape=[jax.ShapeDtypeStruct(momentum.shape, si...  47.4 us

profile of v4, /device:TPU:1, one launch (start us, length us, event | category | flops | bytes accessed | tf_op | source)
XLA Modules:
  0.0 48.7 jit_solution(23597656498194335)
XLA Ops:
  0.6 0.0 copy-start
  0.6 47.4 %shard_map.41 = (f32[6,8,576]{2,1,0:T(8,128)S(1)}, bf16[6,8,640]{2,1,0:T(8,128)(2,1)S(1)}) custom-call(f32[1,6,8,576]{3,2,1,0:T(8,128)} %grads.1, f32[6,8,576]{2,1,0:T(8,128)} %momentum.1), custom_call_target="tpu_custom_call" | custom-call | tf_op jit(solution)/shard_map/pallas_call | solution.py:320
  48.0 0.0 copy-done
  48.0 0.7 %convert_multiply_fusion = (f32[6,8,576]{2,1,0:T(8,128)}, f32[6,8,576]{2,1,0:T(8,128)}) fusion(bf16[6,8,640]{2,1,0:T(8,128)(2,1)S(1)} %get-tuple-element.5, f32[6,8,576]{2,1,0:T(8,128)S(1)} %copy-done, f32[6,8,576]{2,1,0:T(8,128)S(1)} %get-tuple-element.4), kind=kLoop, calls=%fused_computation | loop fusion | flops 138240 | bytes 497664 | tf_op jit(solution)/shard_map/mul | solution.py:359
Async XLA Ops:
  0.6 47.4 %copy-start = (f32[6,8,576]{2,1,0:T(8,128)S(1)}, f32[6,8,576]{2,1,0:T(8,128)}, u32[]{:S(2)}) copy-start(f32[6,8,576]{2,1,0:T(8,128)} %momentum.1) | copy-start | bytes 331780

commit v5 on v4

--- a/solution.py
+++ b/solution.py
@@ -105,7 +105,7 @@
 
     def for_line(act):
         for z_ in range(NZ):
-            for c in range(CORES):
+            for c in (1, 0):
                 if c == 1 and z_ in [hold(j) for j in range(PODS)]:
                     pl.when(z_ != z)(functools.partial(act, z_, c))
                 else:
@@ -118,6 +118,10 @@
 
     along_y = [device(x, lax.rem(y + k, NY), z, 1) for k in ALONG_Y]
     along_x = [device(lax.rem(x + k, NX), y, z, 1) for k in ALONG_X]
+    targets = {}
+    for s in FAR_MATRICES:
+        j = lax.rem(near + s, PODS)
+        targets[s] = (j, device(x, y, hold(j), 1))
     barrier = pltpu.get_barrier_semaphore()
 
     def greet(peer):
@@ -125,7 +129,7 @@
 
     @pl.when(holder)
     def _():
-        for d in range(NZ):
+        for d in (6, 5, 7, 4, 8, 3, 9, 2, 10, 1, 11, 0):
             for c in range(CORES):
                 if (d, c) != (0, 1):
                     greet(device(x, y, lax.rem(z + d, NZ), c))
@@ -135,7 +139,7 @@
     @pl.when(jnp.logical_not(holder))
     def _():
         for s in FAR_MATRICES:
-            greet(device(x, y, hold(lax.rem(near + s, PODS)), 1))
+            greet(targets[s][1])
 
     load_grads.wait()
     load_momentum.wait()
@@ -152,13 +156,13 @@
         pl.semaphore_wait(barrier, PODS)
 
     def term_copy(s):
-        j = lax.rem(near + s, PODS)
+        j, peer = targets[s]
         return remote(
             terms.at[j],
             parts.at[z, core],
             term_send.at[s],
             term_recv.at[z, core],
-            device(x, y, hold(j), 1),
+            peer,
         )
 
     for s in FAR_MATRICES:
@@ -308,6 +312,19 @@
     @pl.when(jnp.logical_not(holder))
     def _():
         term_copy(0).wait_send()
+
+
+def finish(scale, totals, finals, momentum, momentum_out, update_out, first, second, sem):
+    store_update = pltpu.make_async_copy(first, update_out, sem.at[0])
+    store_momentum = pltpu.make_async_copy(second, momentum_out, sem.at[1])
+    first[...] = scale * finals[:, :, : first.shape[-1]].astype(jnp.float32)
+    store_update.start()
+    second[...] = (1 / (1 + momentum_rate)) * totals[...] + (
+        momentum_rate - momentum_rate * momentum_rate / (1 + momentum_rate)
+    ) * momentum[...]
+    store_momentum.start()
+    store_update.wait()
+    store_momentum.wait()
 
 
 def per_device(grads, momentum):
@@ -353,10 +370,18 @@
         pltpu.with_memory_space_constraint(grads, pltpu.HBM),
         pltpu.with_memory_space_constraint(momentum, pltpu.HBM),
     )
-    momentum_new = (1 / (1 + momentum_rate)) * totals + (
-        momentum_rate - momentum_rate * momentum_rate / (1 + momentum_rate)
-    ) * momentum
-    return momentum_new, scale * finals[:, :, :width].astype(single)
+    return pl.pallas_call(
+        functools.partial(finish, scale),
+        out_shape=[jax.ShapeDtypeStruct(momentum.shape, single)] * 2,
+        in_specs=[pl.BlockSpec(memory_space=pltpu.VMEM)] * 3,
+        out_specs=[pl.BlockSpec(memory_space=pltpu.HBM)] * 2,
+        scratch_shapes=[
+            pltpu.VMEM(momentum.shape, single),
+            pltpu.VMEM(momentum.shape, single),
+            dma((2,)),
+        ],
+        compiler_params=pltpu.CompilerParams(vmem_limit_bytes=VMEM_LIMIT),
+    )(totals, finals, momentum)
 
 
 def solution(mesh):

time: 48.9 us -> 48.6 us (level)
  other arithmetic: 0.73 us -> 0 us
    mul x1 -> x0, other arithmetic: 0.73 us -> none  [per_device(): return (momentum_new, scale * finals[:, :, :width].astype(single))]
    pallas_call x0 -> x1, Pallas kernels: none -> 0.72 us  [per_device(): pl.pallas_call(functools.partial(finish, scale), out_shape=[jax.ShapeDtyp...]
where the time goes in v5:
time: 48.6 us; the launch traced here: 48.5 us
  Pallas kernels  47.8 us (98%)
  between operations  0.65 us (1%)
    pallas_call x1, Pallas kernels, per_device(): pl.pallas_call(kernel, out_shape=[jax.ShapeDtypeStruct(momentum.shape, si...  47.1 us

profile of v5, /device:TPU:1, one launch (start us, length us, event | category | flops | bytes accessed | tf_op | source)
XLA Modules:
  0.0 48.5 jit_solution(2285335245950502268)
XLA Ops:
  0.6 0.0 copy-start
  0.6 47.1 %shard_map.41 = (f32[6,8,576]{2,1,0:T(8,128)S(1)}, bf16[6,8,640]{2,1,0:T(8,128)(2,1)S(1)}) custom-call(f32[1,6,8,576]{3,2,1,0:T(8,128)} %grads.1, f32[6,8,576]{2,1,0:T(8,128)} %momentum.3), custom_call_target="tpu_custom_call" | custom-call | tf_op jit(solution)/shard_map/pallas_call | solution.py:337
  47.7 0.0 copy-done
  47.7 0.7 %shard_map.42 = (f32[6,8,576]{2,1,0:T(8,128)}, f32[6,8,576]{2,1,0:T(8,128)}) custom-call(f32[6,8,576]{2,1,0:T(8,128)S(1)} %get-tuple-element.4.totals, bf16[6,8,640]{2,1,0:T(8,128)(2,1)S(1)} %get-tuple-element.5.finals, f32[6,8,576]{2,1,0:T(8,128)S(1)} %copy-done), custom_call_target="tpu_custom_call" | custom-call | tf_op jit(solution)/shard_map/pallas_call | solution.py:373
Async XLA Ops:
  0.6 47.1 %copy-start = (f32[6,8,576]{2,1,0:T(8,128)S(1)}, f32[6,8,576]{2,1,0:T(8,128)}, u32[]{:S(2)}) copy-start(f32[6,8,576]{2,1,0:T(8,128)} %momentum.3) | copy-start | bytes 331780

commit v6 on v5

--- a/solution.py
+++ b/solution.py
@@ -22,13 +22,13 @@
 NY = 8
 CORES = 2
 LANES = 128
-HOLDERS = (0, 2, 3, 5, 8, 10)
+HOLDERS = (0, 1, 3, 5, 9, 10)
 VMEM_LIMIT = 24 << 20
-ALONG_Y = (4, 3, 5, 2, 6, 1, 7)
+ALONG_Y = (4, 5, 3, 6, 2, 7, 1)
 ALONG_X = (1, 3, 2)
 HANDED = {0: 0, 1: 1, 2: 0, 3: 1, 4: 0, 5: 1, 6: 0}
 LAG = 4
-FAR_MATRICES = (3, 2, 4, 1, 5, 0)
+FAR_MATRICES = (3, 4, 2, 5, 1, 0)
 
 
 def hold(j):
@@ -220,14 +220,22 @@
                 x_copy(HANDED[b], b).wait_recv()
                 x_copy(2, b).start()
 
-        for b in range(NY):
-            other = rows.at[0, b]
-            arrived = remote(other, other, y_send.at[0], y_recv.at[b], along_y[0])
-            pl.when(b != place)(arrived.wait_recv)
+        def send_x(b):
             x_copy(0, b).start()
             x_copy(1, b).start()
             if b not in HANDED:
                 x_copy(2, b).start()
+
+        for b in range(NY):
+            pl.when(b == place)(functools.partial(send_x, b))
+
+        def relay(b):
+            other = rows.at[0, b]
+            remote(other, other, y_send.at[0], y_recv.at[b], along_y[0]).wait_recv()
+            send_x(b)
+
+        for b in range(NY):
+            pl.when(b != place)(functools.partial(relay, b))
             pass_on(b - LAG)
         for b in range(NY - LAG, NY):
             pass_on(b)

time: 48.6 us -> 48.2 us (level)
  no operation moved by 1% of the time
where the time goes in v6:
time: 48.2 us; the launch traced here: 48 us
  Pallas kernels  47.4 us (98%)
  between operations  0.65 us (1%)
    pallas_call x1, Pallas kernels, per_device(): pl.pallas_call(kernel, out_shape=[jax.ShapeDtypeStruct(momentum.shape, si...  46.6 us

profile of v6, /device:TPU:1, one launch (start us, length us, event | category | flops | bytes accessed | tf_op | source)
XLA Modules:
  0.0 48.0 jit_solution(15358329665629923211)
XLA Ops:
  0.6 0.0 copy-start
  0.6 46.6 %shard_map.41 = (f32[6,8,576]{2,1,0:T(8,128)S(1)}, bf16[6,8,640]{2,1,0:T(8,128)(2,1)S(1)}) custom-call(f32[1,6,8,576]{3,2,1,0:T(8,128)} %grads.1, f32[6,8,576]{2,1,0:T(8,128)} %momentum.3), custom_call_target="tpu_custom_call" | custom-call | tf_op jit(solution)/shard_map/pallas_call | solution.py:345
  47.3 0.0 copy-done
  47.3 0.7 %shard_map.42 = (f32[6,8,576]{2,1,0:T(8,128)}, f32[6,8,576]{2,1,0:T(8,128)}) custom-call(f32[6,8,576]{2,1,0:T(8,128)S(1)} %get-tuple-element.4.totals, bf16[6,8,640]{2,1,0:T(8,128)(2,1)S(1)} %get-tuple-element.5.finals, f32[6,8,576]{2,1,0:T(8,128)S(1)} %copy-done), custom_call_target="tpu_custom_call" | custom-call | tf_op jit(solution)/shard_map/pallas_call | solution.py:381
Async XLA Ops:
  0.6 46.7 %copy-start = (f32[6,8,576]{2,1,0:T(8,128)S(1)}, f32[6,8,576]{2,1,0:T(8,128)}, u32[]{:S(2)}) copy-start(f32[6,8,576]{2,1,0:T(8,128)} %momentum.3) | copy-start | bytes 331780

commit v7 on v6

--- a/solution.py
+++ b/solution.py
@@ -26,7 +26,7 @@
 VMEM_LIMIT = 24 << 20
 ALONG_Y = (4, 5, 3, 6, 2, 7, 1)
 ALONG_X = (1, 3, 2)
-HANDED = {0: 0, 1: 1, 2: 0, 3: 1, 4: 0, 5: 1, 6: 0}
+HANDED = {0: 0, 1: 1, 2: 0, 3: 1, 4: 0, 5: 1, 6: 0, 7: 1}
 LAG = 4
 FAR_MATRICES = (3, 4, 2, 5, 1, 0)
 
@@ -268,9 +268,15 @@
         inverse = 1.0 / (jnp.sqrt(trace) + epsilon)
         gram = (raw[...] * (inverse * inverse)).astype(jnp.bfloat16)
         start = (rows[0, place].astype(jnp.float32) * inverse).astype(jnp.bfloat16)
-        polynomial = (
-            coef_b * gram.astype(jnp.float32) + coef_c * dot(gram, gram)
-        ).astype(jnp.bfloat16)
+        polynomial = jnp.concatenate(
+            [
+                (
+                    coef_b * gram[:width].astype(jnp.float32) + coef_c * dot(gram[:width], gram)
+                ).astype(jnp.bfloat16),
+                jnp.zeros((wide - width, wide), jnp.bfloat16),
+            ],
+            axis=0,
+        )
 
         def step(value):
             return coef_a * value + dot(value.astype(jnp.bfloat16), polynomial)

time: 48.2 us -> 49.1 us (1.019)
  Pallas kernels: 47.4 us -> 48.3 us
    pallas_call x1, Pallas kernels: 46.6 us -> 47.6 us  [per_device(): pl.pallas_call(kernel, out_shape=[jax.ShapeDtypeStruct(momentum.shape, si...]
where the time goes in v7:
time: 49.1 us; the launch traced here: 49 us
  Pallas kernels  48.3 us (98%)
  between operations  0.65 us (1%)
    pallas_call x1, Pallas kernels, per_device(): pl.pallas_call(kernel, out_shape=[jax.ShapeDtypeStruct(momentum.shape, si...  47.6 us

profile of v7, /device:TPU:1, one launch (start us, length us, event | category | flops | bytes accessed | tf_op | source)
XLA Modules:
  0.0 49.0 jit_solution(9532662306146725499)
XLA Ops:
  0.6 0.0 copy-start
  0.6 47.6 %shard_map.41 = (f32[6,8,576]{2,1,0:T(8,128)S(1)}, bf16[6,8,640]{2,1,0:T(8,128)(2,1)S(1)}) custom-call(f32[1,6,8,576]{3,2,1,0:T(8,128)} %grads.1, f32[6,8,576]{2,1,0:T(8,128)} %momentum.3), custom_call_target="tpu_custom_call" | custom-call | tf_op jit(solution)/shard_map/pallas_call | solution.py:351
  48.2 0.0 copy-done
  48.2 0.7 %shard_map.42 = (f32[6,8,576]{2,1,0:T(8,128)}, f32[6,8,576]{2,1,0:T(8,128)}) custom-call(f32[6,8,576]{2,1,0:T(8,128)S(1)} %get-tuple-element.4.totals, bf16[6,8,640]{2,1,0:T(8,128)(2,1)S(1)} %get-tuple-element.5.finals, f32[6,8,576]{2,1,0:T(8,128)S(1)} %copy-done), custom_call_target="tpu_custom_call" | custom-call | tf_op jit(solution)/shard_map/pallas_call | solution.py:387
Async XLA Ops:
  0.6 47.6 %copy-start = (f32[6,8,576]{2,1,0:T(8,128)S(1)}, f32[6,8,576]{2,1,0:T(8,128)}, u32[]{:S(2)}) copy-start(f32[6,8,576]{2,1,0:T(8,128)} %momentum.3) | copy-start | bytes 331780
